TPU v7x, 32 devices: a whole 2x2x4 slice. The times are simulated.
32 devices in a mesh: rows: 8 (over z, x), tm: 4 (over y, core).
Axes of the slice: x: 2, y: 2, z: 4, core: 2. Of those that a mesh axis runs over, the one named last changes fastest.
Arguments:
- snapshots: bfloat16 [262144, 512], P('rows', 'tm'), may hold values from -6 to 6
- modes: bfloat16 [262144, 256], P('rows'), may hold values from -0.01171875 to 0.01171875
- eig_vectors: float32 [3, 256], replicated, may hold values from -0.375 to 0.375
- eig_values: float32 [3], replicated, may hold values from -1 to 1
Outputs:
- operator: float32 [256, 256], replicated
- eig_residual: float32 [3, 256], replicated
- residual_norm: float32 [3], replicated
All inputs are finite; a program needn't handle non-finite values.
Results may differ from a plain program's by a relative error of at most 0.0003.
Values may be sent and summed in bfloat16 or wider, within the bound.
A program may use at most 128 MiB of HBM per device.

v0:
```python
import jax
import jax.numpy as jnp
from jax import lax
from jax.sharding import PartitionSpec as P


def pair_terms(coords, after, keep):
    lead = coords * keep
    trail = jnp.concatenate([coords[:, 1:], after], axis=1)
    cross_part = jnp.dot(
        trail, lead.T, precision=lax.Precision.HIGHEST, preferred_element_type=jnp.float32
    )
    gram_part = jnp.dot(
        lead, lead.T, precision=lax.Precision.HIGHEST, preferred_element_type=jnp.float32
    )
    return (cross_part, gram_part)


def body(snapshots, modes, eig_vectors, eig_values):
    block_cols = snapshots.shape[1]
    width = modes.shape[1]
    time_count = lax.axis_size("tm")
    total_cols = block_cols * time_count
    partial_value = jnp.einsum("mr,mt->rt", modes, snapshots, preferred_element_type=jnp.float32)
    coords = lax.psum(partial_value, "rows")
    series = lax.all_gather(coords, "tm", axis=1, tiled=True)
    every = lax.broadcasted_iota(jnp.int32, (1, total_cols), 1)
    whole_keep = (every < total_cols - 1).astype(jnp.float32)
    zero_col = jnp.zeros((width, 1), jnp.float32)
    cross, gram = pair_terms(series, zero_col, whole_keep)
    scale = jnp.float32(total_cols - 1)
    cross = cross / scale
    gram = gram / scale + jnp.eye(width, dtype=jnp.float32)
    factor = jnp.linalg.cholesky(gram)
    operator = jax.scipy.linalg.cho_solve((factor, True), cross.T).T
    eig_residual = (
        jnp.dot(
            eig_vectors,
            operator.T,
            precision=lax.Precision.HIGHEST,
            preferred_element_type=jnp.float32,
        )
        - eig_values[:, None] * eig_vectors
    )
    residual_norm = jnp.sqrt(jnp.sum(eig_residual * eig_residual, axis=1) + 1e-06)
    return (operator, eig_residual, residual_norm)


def solution(mesh):
    return jax.shard_map(
        body,
        mesh=mesh,
        in_specs=(P("rows", "tm"), P("rows", None), P(), P()),
        out_specs=(P(), P(), P()),
        check_vma=False,
    )
```

profile of v0, /device:TPU:0, one launch (start us, length us, event | category | flops | bytes accessed | tf_op | source)
XLA Modules:
  0.0 174.0 jit_solution(5392952128399339872)
XLA Ops:
  7.2 0.0 copy-start
  7.2 0.0 copy-start.1
  7.2 0.0 all-reduce.4.cloned.1.call-start
  7.2 13.4 %fusion.23 = f32[256,128]{1,0:T(8,128)} fusion(bf16[32768,256]{1,0:T(8,128)(2,1)} %param.5, bf16[32768,128]{1,0:T(8,128)(2,1)} %param.4), kind=kOutput, calls=%fused_computation.53 | convolution fusion | flops 2147483648 | bytes 25296896 | tf_op jit(solution)/shard_map/mr,mt->rt/dot_general | solution.py:24
  20.6 0.0 all-reduce.4.cloned.1.call-update
  20.7 73.3 %all-reduce.4.cloned.1.call-done = f32[256,128]{1,0:T(8,128)} async-done(((f32[256,128]{1,0:T(8,128)}), f32[256,128]{1,0:T(8,128)}) %all-reduce.4.cloned.1.call-update) | async-done | bytes 131088 | tf_op jit(solution)/shard_map/psum | solution.py:25
  94.0 7.5 %all_gather.3 = f32[256,512]{1,0:T(8,128)S(1)} all-gather(f32[256,128]{1,0:T(8,128)} %all-reduce.4.cloned.1.call-done), channel_id=1, replica_groups=mesh['rows'=8,'tm'=4] {'tm'}, dimensions={1}, use_global_device_ids=true | all-gather | bytes 655360 | tf_op jit(solution)/shard_map/all_gather | solution.py:26
  101.5 0.2 slice.77
  101.7 0.6 convert_add_fusion
  102.4 0.6 convolution_multiply_fusion
  103.0 0.1 copy.8
  103.2 11.7 %cholesky.50 = f32[128,128]{1,0:T(8,128)S(1)} custom-call(f32[128,128]{1,0:T(8,128)S(1)} %cholesky.118), custom_call_target="Cholesky" | custom-call | tf_op jit(solution)/shard_map/jit(cholesky)/cholesky | solution.py:34
  115.0 9.8 %custom-call.18 = f32[1,128,128]{1,2,0:T(8,128)S(1)} custom-call(f32[1,128,128]{2,1,0:T(8,128)S(1)} %get-tuple-element.27), custom_call_target="InvertDiagBlocksLowerTriangular" | custom-call | tf_op jit(solution)/shard_map/jit(cholesky)/cholesky | solution.py:34
  124.8 0.2 constant_dynamic-update-slice_fusion.1
  125.0 0.3 convolution_subtract_fusion.2
  125.3 11.7 %cholesky.105 = f32[128,128]{1,0:T(8,128)S(1)} custom-call(f32[128,128]{1,0:T(8,128)S(1)} %convolution_subtract_fusion.2), custom_call_target="Cholesky" | custom-call | tf_op jit(solution)/shard_map/jit(cholesky)/cholesky | solution.py:34
  137.0 0.6 compare_reduce_fusion
  139.0 0.1 triangular_solve.72
  139.1 4.2 %while.1 = (s32[]{:T(128)}, f32[256,256]{1,0:T(8,128)S(1)}, s32[2,2]{1,0:T(2,128)S(1)}, f32[2,128,128]{2,1,0:T(8,128)S(1)}, s32[]{:T(128)}) while((s32[]{:T(128)}, f32[256,256]{1,0:T(8,128)S(1)}, s32[2,2]{1,0:T(2,128)S(1)}, f32[2,128,128]{2,1,0:T(8,128)S(1)}, s32[]{:T(128)}) %tuple.30), condition=%wide.while_cond, body=%wide.while_body.sunk | while | flops 2 | bytes 131189 | solution.py:35
  139.3 0.6 fusion.35
  139.9 1.4 bitcast_dynamic-update-slice_fusion.2
  141.3 0.6 fusion.35
  141.9 1.4 bitcast_dynamic-update-slice_fusion.2
  143.3 19.7 %custom-call.19 = f32[2,128,128]{1,2,0:T(8,128)S(1)} custom-call(f32[2,128,128]{2,1,0:T(8,128)S(1)} %get-tuple-element.10), custom_call_target="InvertDiagBlocksLowerTriangular" | custom-call | tf_op jit(solution)/shard_map/jit(_cho_solve)/triangular_solve | solution.py:35
  162.9 0.3 fusion.9
  163.3 0.4 convolution_subtract_fusion.1
  163.7 0.3 fusion.16
  164.0 0.3 fusion.15
  164.2 0.3 convolution_subtract_fusion
  164.6 0.3 fusion.14
  164.9 0.8 copy.10
  165.7 0.0 copy-done
  165.7 0.0 copy-done.1
  165.7 1.0 multiply_reduce_fusion
  166.7 0.5 add_sqrt_fusion
  (12 shorter events, 0.2 us)
Async XLA Ops:
  7.2 158.5 %copy-start = (f32[3,256]{1,0:T(4,128)S(1)}, f32[3,256]{1,0:T(4,128)}, u32[]{:S(2)}) copy-start(f32[3,256]{1,0:T(4,128)} %param.6) | copy-start | bytes 9220
  7.2 158.5 %copy-start.1 = (f32[3]{0:T(128)S(1)}, f32[3]{0:T(128)}, u32[]{:S(2)}) copy-start(f32[3]{0:T(128)} %param.7) | copy-start | bytes 40
  7.2 86.8 %all-reduce.4.cloned.1.call-start = ((), (), s32[]{:S(2)}) async-start(), calls=%async_computation | async-start | bytes 262144 | tf_op jit(solution)/shard_map/psum | solution.py:25
Sparse Core Ops, SparseCore 0:
  20.8 73.1 all-reduce.3
where the time goes:
time: 174 us
  waiting for transfers between devices  73.3 us (42%)
  other arithmetic  54.2 us (31%)
  matrix products  17.9 us (10%)
  between operations  15.5 us (9%)
  blocking collectives  7.53 us (4%)
  local copies, waits for them, and re-layouts  5.22 us (3%)
    psum x1, waiting for transfers between devices, body(): coords = lax.psum(partial_value, 'rows')  73.3 us
    another operation x6, other arithmetic, body(): factor = jnp.linalg.cholesky(gram)  33.9 us
    another operation x3, other arithmetic, body(): operator = jax.scipy.linalg.cho_solve((factor, True), cross.T).T  19.7 us
    dot_general x1, matrix products, body(): jnp.einsum('mr,mt->rt', modes, snapshots, preferred_element_type=jnp.floa...  13.4 us
    all_gather x1, blocking collectives, body(): series = lax.all_gather(coords, 'tm', axis=1, tiled=True)  7.53 us
    another operation x6, local copies, waits for them, and re-layouts  3.95 us
  transfers between devices with their start and end apart: 1, of which 1 were waited for; matrix products, arithmetic and copies ran while one was open for 0% of the time, Pallas kernels for 0%

commit v1 on v0

--- a/solution.py
+++ b/solution.py
@@ -22,7 +22,9 @@
     time_count = lax.axis_size("tm")
     total_cols = block_cols * time_count
     partial_value = jnp.einsum("mr,mt->rt", modes, snapshots, preferred_element_type=jnp.float32)
-    coords = lax.psum(partial_value, "rows")
+    coords = partial_value
+    for hop in (1, 2, 4):
+        coords = coords + lax.ppermute(coords, "rows", [(dev, dev ^ hop) for dev in range(8)])
     series = lax.all_gather(coords, "tm", axis=1, tiled=True)
     every = lax.broadcasted_iota(jnp.int32, (1, total_cols), 1)
     whole_keep = (every < total_cols - 1).astype(jnp.float32)

time: 174 us -> 104 us (0.60)
  waiting for transfers between devices: 73.3 us -> 11.1 us
  between operations: 15.5 us -> 2.12 us
  starting transfers between devices: 0.04 us -> 7.82 us
  matrix products: 17.9 us -> 15.1 us
    psum x1 -> x0, waiting for transfers between devices: 73.3 us -> none  [body(): coords = lax.psum(partial_value, 'rows')]
    ppermute x0 -> x3, waiting for transfers between devices: none -> 11.1 us  [body(): lax.ppermute(coords, 'rows', [(dev, dev ^ hop) for dev in range(8)])]
    ppermute x0 -> x3, starting transfers between devices: none -> 7.82 us  [body(): lax.ppermute(coords, 'rows', [(dev, dev ^ hop) for dev in range(8)])]
    dot_general x1, matrix products: 13.4 us -> 10.6 us  [body(): jnp.einsum('mr,mt->rt', modes, snapshots, preferred_element_type=jnp.floa...]
  transfers between devices with their start and end apart: 1 -> 3, of which waited for: 1 -> 3; matrix products, arithmetic and copies ran while one was open for 0% -> 0% of each run, Pallas kernels for 0% -> 0%
where the time goes in v1:
time: 104 us; the launch traced here: 103 us
  other arithmetic  54.3 us (52%)
  matrix products  15.1 us (15%)
  waiting for transfers between devices  11.1 us (11%)
  starting transfers between devices  7.82 us (8%)
  blocking collectives  7.63 us (7%)
  local copies, waits for them, and re-layouts  5.22 us (5%)
  between operations  2.12 us (2%)
    another operation x6, other arithmetic, body(): factor = jnp.linalg.cholesky(gram)  33.9 us
    another operation x3, other arithmetic, body(): operator = jax.scipy.linalg.cho_solve((factor, True), cross.T).T  19.7 us
    ppermute x3, waiting for transfers between devices, body(): lax.ppermute(coords, 'rows', [(dev, dev ^ hop) for dev in range(8)])  11.1 us
    dot_general x1, matrix products, body(): jnp.einsum('mr,mt->rt', modes, snapshots, preferred_element_type=jnp.floa...  10.6 us
    ppermute x3, starting transfers between devices, body(): lax.ppermute(coords, 'rows', [(dev, dev ^ hop) for dev in range(8)])  7.82 us
    all_gather x1, blocking collectives, body(): series = lax.all_gather(coords, 'tm', axis=1, tiled=True)  7.63 us
    another operation x6, local copies, waits for them, and re-layouts  3.95 us
  transfers between devices with their start and end apart: 3, of which 3 were waited for; matrix products, arithmetic and copies ran while one was open for 0% of the time, Pallas kernels for 0%

profile of v1, /device:TPU:0, one launch (start us, length us, event | category | flops | bytes accessed | tf_op | source)
XLA Modules:
  0.0 103.5 jit_solution(17278030177177012005)
XLA Ops:
  0.6 0.0 copy-start
  0.6 0.0 copy-start.1
  0.7 10.6 %fusion.24 = f32[256,128]{1,0:T(8,128)S(1)} fusion(bf16[32768,256]{1,0:T(8,128)(2,1)} %param.5, bf16[32768,128]{1,0:T(8,128)(2,1)} %param.4), kind=kOutput, calls=%fused_computation.54 | convolution fusion | flops 2147483648 | bytes 25296896 | tf_op jit(solution)/shard_map/mr,mt->rt/dot_general | solution.py:24
  11.3 3.0 %collective-permute-start = (f32[256,128]{1,0:T(8,128)S(1)}, f32[256,128]{1,0:T(8,128)S(1)}, u32[]{:S(2)}, u32[]{:S(2)}) collective-permute-start(f32[256,128]{1,0:T(8,128)S(1)} %fusion.24), channel_id=1, source_target_pairs={{0,4},{4,0},{8,12},{12,8},{16,20},{20,16},{24,28},{28,24},{1,5},{5... | collective-permute-start | bytes 393224 | tf_op jit(solution)/shard_map/ppermute | solution.py:27
  14.3 3.5 %collective-permute-done = f32[256,128]{1,0:T(8,128)S(1)} collective-permute-done((f32[256,128]{1,0:T(8,128)S(1)}, f32[256,128]{1,0:T(8,128)S(1)}, u32[]{:S(2)}, u32[]{:S(2)}) %collective-permute-start) | collective-permute-done | bytes 131104 | tf_op jit(solution)/shard_map/ppermute | solution.py:27
  17.8 1.9 %collective-permute-start.1 = (f32[256,128]{1,0:T(8,128)S(1)}, f32[256,128]{1,0:T(8,128)S(1)}, u32[]{:S(2)}, u32[]{:S(2)}) collective-permute-start(f32[256,128]{1,0:T(8,128)S(1)} %add.46), channel_id=1, source_target_pairs={{0,8},{4,12},{8,0},{12,4},{16,24},{20,28},{24,16},{28,20},{1,9},{5... | collective-permute-start | bytes 393224 | tf_op jit(solution)/shard_map/ppermute | solution.py:27
  19.7 3.1 %collective-permute-done.1 = f32[256,128]{1,0:T(8,128)S(1)} collective-permute-done((f32[256,128]{1,0:T(8,128)S(1)}, f32[256,128]{1,0:T(8,128)S(1)}, u32[]{:S(2)}, u32[]{:S(2)}) %collective-permute-start.1) | collective-permute-done | bytes 131104 | tf_op jit(solution)/shard_map/ppermute | solution.py:27
  22.9 2.9 %collective-permute-start.2 = (f32[256,128]{1,0:T(8,128)S(1)}, f32[256,128]{1,0:T(8,128)S(1)}, u32[]{:S(2)}, u32[]{:S(2)}) collective-permute-start(f32[256,128]{1,0:T(8,128)S(1)} %add.47), channel_id=1, source_target_pairs={{0,16},{4,20},{8,24},{12,28},{16,0},{20,4},{24,8},{28,12},{1,17},{... | collective-permute-start | bytes 393224 | tf_op jit(solution)/shard_map/ppermute | solution.py:27
  25.8 4.4 %collective-permute-done.2 = f32[256,128]{1,0:T(8,128)S(1)} collective-permute-done((f32[256,128]{1,0:T(8,128)S(1)}, f32[256,128]{1,0:T(8,128)S(1)}, u32[]{:S(2)}, u32[]{:S(2)}) %collective-permute-start.2) | collective-permute-done | bytes 131104 | tf_op jit(solution)/shard_map/ppermute | solution.py:27
  30.2 7.6 %all_gather.3 = f32[256,512]{1,0:T(8,128)S(1)} all-gather(f32[256,128]{1,0:T(8,128)S(1)} %add.48), channel_id=1, replica_groups=mesh['rows'=8,'tm'=4] {'tm'}, dimensions={1}, use_global_device_ids=true | all-gather | bytes 655360 | tf_op jit(solution)/shard_map/all_gather | solution.py:28
  37.8 0.2 slice.77
  38.0 0.6 convert_add_fusion
  38.7 0.6 convolution_multiply_fusion
  39.3 0.1 copy.8
  39.5 11.7 %cholesky.50 = f32[128,128]{1,0:T(8,128)S(1)} custom-call(f32[128,128]{1,0:T(8,128)S(1)} %cholesky.118), custom_call_target="Cholesky" | custom-call | tf_op jit(solution)/shard_map/jit(cholesky)/cholesky | solution.py:36
  51.3 9.8 %custom-call.18 = f32[1,128,128]{1,2,0:T(8,128)S(1)} custom-call(f32[1,128,128]{2,1,0:T(8,128)S(1)} %get-tuple-element.27), custom_call_target="InvertDiagBlocksLowerTriangular" | custom-call | tf_op jit(solution)/shard_map/jit(cholesky)/cholesky | solution.py:36
  61.1 0.2 constant_dynamic-update-slice_fusion.1
  61.3 0.3 convolution_subtract_fusion.1
  61.6 11.7 %cholesky.105 = f32[128,128]{1,0:T(8,128)S(1)} custom-call(f32[128,128]{1,0:T(8,128)S(1)} %convolution_subtract_fusion.1), custom_call_target="Cholesky" | custom-call | tf_op jit(solution)/shard_map/jit(cholesky)/cholesky | solution.py:36
  73.3 0.6 compare_reduce_fusion
  75.3 0.1 triangular_solve.72
  75.4 4.2 %while.1 = (s32[]{:T(128)}, f32[256,256]{1,0:T(8,128)S(1)}, s32[2,2]{1,0:T(2,128)S(1)}, f32[2,128,128]{2,1,0:T(8,128)S(1)}, s32[]{:T(128)}) while((s32[]{:T(128)}, f32[256,256]{1,0:T(8,128)S(1)}, s32[2,2]{1,0:T(2,128)S(1)}, f32[2,128,128]{2,1,0:T(8,128)S(1)}, s32[]{:T(128)}) %tuple.30), condition=%wide.while_cond, body=%wide.while_body.sunk | while | flops 2 | bytes 131189 | solution.py:37
  75.6 0.6 fusion.35
  76.2 1.4 %bitcast_dynamic-update-slice_fusion.2 = f32[2,128,128]{2,1,0:T(8,128)S(1)} fusion(f32[2,128,128]{2,1,0:T(8,128)S(1)} %get-tuple-element.73, s32[]{:T(128)S(6)} %copy.18, f32[256,256]{1,0:T(8,128)S(1)} %get-tuple-element.76, s32[]{:T(128)} %bitcast.44, s32[]{:T(128)} %bitcast.45), kind=kLoop, calls=%fused_computation.clone.1 | loop fusion | bytes 131084 | tf_op jit(solution)/shard_map/jit(_cho_solve)/triangular_solve
  77.6 0.6 fusion.35
  78.2 1.4 %bitcast_dynamic-update-slice_fusion.2 = f32[2,128,128]{2,1,0:T(8,128)S(1)} fusion(f32[2,128,128]{2,1,0:T(8,128)S(1)} %get-tuple-element.73, s32[]{:T(128)S(6)} %copy.18, f32[256,256]{1,0:T(8,128)S(1)} %get-tuple-element.76, s32[]{:T(128)} %bitcast.44, s32[]{:T(128)} %bitcast.45), kind=kLoop, calls=%fused_computation.clone.1 | loop fusion | bytes 131084 | tf_op jit(solution)/shard_map/jit(_cho_solve)/triangular_solve
  79.6 19.7 %custom-call.19 = f32[2,128,128]{1,2,0:T(8,128)S(1)} custom-call(f32[2,128,128]{2,1,0:T(8,128)S(1)} %get-tuple-element.10), custom_call_target="InvertDiagBlocksLowerTriangular" | custom-call | tf_op jit(solution)/shard_map/jit(_cho_solve)/triangular_solve | solution.py:37
  99.2 0.3 fusion.10
  99.6 0.4 fusion.18
  100.0 0.3 fusion.9
  100.3 0.3 fusion.16
  100.5 0.3 convolution_subtract_fusion
  100.9 0.3 fusion.15
  101.2 0.8 copy.10
  102.0 0.0 copy-done
  102.0 0.0 copy-done.1
  102.0 1.0 multiply_reduce_fusion
  103.0 0.5 add_sqrt_fusion
  (15 shorter events, 0.3 us)
Async XLA Ops:
  0.6 101.4 %copy-start = (f32[3,256]{1,0:T(4,128)S(1)}, f32[3,256]{1,0:T(4,128)}, u32[]{:S(2)}) copy-start(f32[3,256]{1,0:T(4,128)} %param.6) | copy-start | bytes 9220
  0.6 101.4 %copy-start.1 = (f32[3]{0:T(128)S(1)}, f32[3]{0:T(128)}, u32[]{:S(2)}) copy-start(f32[3]{0:T(128)} %param.7) | copy-start | bytes 40
  11.3 6.5 %collective-permute-start = (f32[256,128]{1,0:T(8,128)S(1)}, f32[256,128]{1,0:T(8,128)S(1)}, u32[]{:S(2)}, u32[]{:S(2)}) collective-permute-start(f32[256,128]{1,0:T(8,128)S(1)} %fusion.24), channel_id=1, source_target_pairs={{0,4},{4,0},{8,12},{12,8},{16,20},{20,16},{24,28},{28,24},{1,5},{5... | collective-permute-start | bytes 393224 | tf_op jit(solution)/shard_map/ppermute | solution.py:27
  17.8 5.0 %collective-permute-start.1 = (f32[256,128]{1,0:T(8,128)S(1)}, f32[256,128]{1,0:T(8,128)S(1)}, u32[]{:S(2)}, u32[]{:S(2)}) collective-permute-start(f32[256,128]{1,0:T(8,128)S(1)} %add.46), channel_id=1, source_target_pairs={{0,8},{4,12},{8,0},{12,4},{16,24},{20,28},{24,16},{28,20},{1,9},{5... | collective-permute-start | bytes 393224 | tf_op jit(solution)/shard_map/ppermute | solution.py:27
  22.9 7.3 %collective-permute-start.2 = (f32[256,128]{1,0:T(8,128)S(1)}, f32[256,128]{1,0:T(8,128)S(1)}, u32[]{:S(2)}, u32[]{:S(2)}) collective-permute-start(f32[256,128]{1,0:T(8,128)S(1)} %add.47), channel_id=1, source_target_pairs={{0,16},{4,20},{8,24},{12,28},{16,0},{20,4},{24,8},{28,12},{1,17},{... | collective-permute-start | bytes 393224 | tf_op jit(solution)/shard_map/ppermute | solution.py:27
